TPU v7x, 128 devices: a whole 4x4x4 slice. The times are simulated.
128 devices in a mesh: layer: 4 (over x_hi, core), feat: 16 (over z, y), par: 2 (over x_lo).
Axes of the slice: x: 4 (x_hi: 2, x_lo: 2; x = x_hi * 2 + x_lo), y: 4, z: 4, core: 2. Of those that a mesh axis runs over, the one named last changes fastest.
Arguments:
- residual: bfloat16 [4, 512, 2304], P('layer'), may hold values from -6 to 6
- norm_gain: float32 [4, 2304], P('layer'), may hold values from 0.5 to 1.5
- gate_weight: bfloat16 [4, 2304, 9216], P('layer', None, ('feat', 'par')), may hold values from -0.125 to 0.125
- up_weight: bfloat16 [4, 2304, 9216], P('layer', None, ('feat', 'par')), may hold values from -0.125 to 0.125
- down_weight: bfloat16 [4, 9216, 2304], P('layer', ('feat', 'par')), may hold values from -0.0625 to 0.0625
- enc_weight: float32 [4, 2304, 8192], P('layer', 'par', 'feat'), may hold values from -0.125 to 0.125
- enc_bias: float32 [4, 8192], P('layer', 'feat'), may hold values from -1 to 0.5
- dec_weight: bfloat16 [4, 2, 2, 8192, 2304], P('layer', 'par', None, 'feat'), may hold values from -0.0625 to 0.0625
- dec_bias: float32 [4, 2304], replicated, may hold values from -3 to 3
Outputs:
- enc_grad: float32 [4, 2304, 8192], P('layer', 'par', 'feat')
- enc_bias_grad: float32 [4, 8192], P('layer', 'feat')
- dec_grad: bfloat16 [4, 2, 2, 8192, 2304], P('layer', 'par', None, 'feat')
All inputs are finite; a program needn't handle non-finite values.
Results may differ from a plain program's by a relative error of at most 0.007.
Values may be sent and summed in bfloat16 or wider, within the bound.
A program may use at most 192 MiB of HBM per device.

v0:
```python
import jax
import jax.numpy as jnp
from jax import lax
from jax.sharding import PartitionSpec as P


def rms_normed(rows_in, gain_row):
    values = rows_in.astype(jnp.float32)
    scaling = lax.rsqrt(jnp.mean(values * values, axis=-1, keepdims=True) + 1e-06)
    return (values * scaling * gain_row).astype(jnp.bfloat16)


def shards(
    residual,
    norm_gain,
    gate_weight,
    up_weight,
    down_weight,
    enc_weight,
    enc_bias,
    dec_weight,
    dec_bias,
):
    highest = lax.Precision.HIGHEST
    source = lax.axis_index("layer")
    parity = lax.axis_index("par")
    slot_count = dec_weight.shape[2]
    normed = rms_normed(residual[0], norm_gain[0])
    tokens, model_width = normed.shape
    gate_value = jnp.dot(normed, gate_weight[0], preferred_element_type=jnp.float32)
    up_value = jnp.dot(normed, up_weight[0], preferred_element_type=jnp.float32)
    hidden = (jax.nn.gelu(gate_value, approximate=True) * up_value).astype(jnp.bfloat16)
    target_part = jnp.dot(hidden, down_weight[0], preferred_element_type=jnp.float32)
    half_width = enc_weight.shape[1]
    my_rows = lax.dynamic_slice_in_dim(normed, parity * half_width, half_width, 1).astype(
        jnp.float32
    )
    pre_part = jnp.dot(my_rows, enc_weight[0], precision=highest)
    pre_act = lax.psum(pre_part, "par") + enc_bias[0]
    positive = jnp.maximum(pre_act, 0.0)
    actives = (positive * positive).astype(jnp.bfloat16)
    slot_ids = jnp.arange(slot_count, dtype=jnp.int32)
    slot_live = 2 * slot_ids + parity >= source
    live_float = slot_live.astype(jnp.float32)
    decoders = dec_weight[0, 0]
    recon_parts = (
        jnp.einsum("tf,jfd->jtd", actives, decoders, preferred_element_type=jnp.float32)
        * live_float[:, None, None]
    )
    bias_slots = lax.dynamic_index_in_dim(
        dec_bias.reshape(slot_count, 2, model_width), parity, 1, keepdims=False
    )
    full_target = lax.psum(target_part, ("feat", "par"))
    all_targets = lax.all_gather(full_target[None], "layer", axis=0, tiled=True)
    target_slots = lax.dynamic_index_in_dim(
        all_targets.reshape(slot_count, 2, tokens, model_width), parity, 1, keepdims=False
    )
    summed_rows = lax.psum(recon_parts, ("layer", "feat"))
    err_full = summed_rows + bias_slots[:, None, :]
    err_full = err_full - target_slots
    errors = (err_full * 0.0625).astype(jnp.bfloat16)
    masked = errors * slot_live.astype(jnp.bfloat16)[:, None, None]
    back_part = jnp.einsum("jtd,jfd->tf", masked, decoders, preferred_element_type=jnp.float32)
    back_grad = lax.psum(back_part.astype(jnp.bfloat16), "par").astype(jnp.float32)
    d_pre = back_grad * 2.0 * positive
    enc_grad = lax.dot_general(my_rows, d_pre, (((0,), (0,)), ((), ())), precision=highest)
    bias_grad = jnp.sum(d_pre, axis=0)
    dec_grad = jnp.einsum(
        "tf,jtd->jfd", actives, masked, preferred_element_type=jnp.float32
    ).astype(jnp.bfloat16)
    return (enc_grad[None], bias_grad[None], dec_grad[None, None])


def solution(mesh):
    return jax.shard_map(
        shards,
        mesh=mesh,
        in_specs=(
            P("layer", None, None),
            P("layer", None),
            P("layer", None, ("feat", "par")),
            P("layer", None, ("feat", "par")),
            P("layer", ("feat", "par"), None),
            P("layer", "par", "feat"),
            P("layer", "feat"),
            P("layer", "par", None, "feat", None),
            P(),
        ),
        out_specs=(
            P("layer", "par", "feat"),
            P("layer", "feat"),
            P("layer", "par", None, "feat", None),
        ),
        check_vma=False,
    )
```

profile of v0, /device:TPU:1, one launch (start us, length us, event | category | flops | bytes accessed | tf_op | source)
XLA Modules:
  0.0 1276.6 jit_solution(10719600831375024537)
XLA Ops:
  7.2 0.0 all-reduce.5.cloned.1.call-start
  7.2 2.4 multiply_reduce_fusion
  9.6 4.2 convert_bitcast_fusion
  13.8 0.1 dynamic-slice
  13.9 4.9 fusion.12
  18.8 0.0 all-reduce.5.cloned.1.call-update
  18.9 0.0 all-reduce.9.cloned.1.call-start
  18.9 3.2 fusion.43
  22.2 6.3 convolution_bitcast_fusion
  28.5 0.0 all-reduce.7.cloned.1.call-start
  28.5 40.3 %all-reduce.5.cloned.1.call-done = f32[512,512]{1,0:T(8,128)} async-done(((f32[512,512]{1,0:T(8,128)}), f32[512,512]{1,0:T(8,128)}) %all-reduce.5.cloned.1.call-update) | async-done | bytes 1048592 | tf_op jit(solution)/shard_map/psum | solution.py:39
  68.8 8.9 multiply_bitcast_fusion
  77.8 0.0 all-gather.2.cloned.1.call-start
  77.8 314.6 %all-reduce.9.cloned.1.call-done = f32[1,512,2304]{2,1,0:T(8,128)} async-done(((f32[1,512,2304]{2,1,0:T(8,128)}), f32[1,512,2304]{2,1,0:T(8,128)}) %all-reduce.9.cloned.1.call-update) | async-done | bytes 4718608 | tf_op jit(solution)/shard_map/psum | solution.py:53
  392.5 0.2 all-reduce.11.cloned.1.call-start
  392.8 668.2 %all-reduce.7.cloned.1.call-done = f32[2,512,2304]{2,1,0:T(8,128)} async-done(((f32[2,512,2304]{2,1,0:T(8,128)}), f32[2,512,2304]{2,1,0:T(8,128)}) %all-reduce.7.cloned.1.call-update) | async-done | bytes 9437200 | tf_op jit(solution)/shard_map/psum | solution.py:58
  1061.0 149.9 %all-gather.2.cloned.1.call-done = f32[4,512,2304]{2,1,0:T(8,128)} async-done(((f32[1,512,2304]{2,1,0:T(8,128)}), f32[4,512,2304]{2,1,0:T(8,128)}) %all-gather.2.cloned.1.call-update) | async-done | bytes 18874384 | tf_op jit(solution)/shard_map/all_gather | solution.py:54
  1210.8 10.1 fusion.5
  1220.9 7.3 fusion.22
  1228.2 6.7 fusion.2
  1234.9 6.8 copy.17
  1241.7 21.0 %all-reduce.11.cloned.1.call-done = bf16[512,512]{1,0:T(8,128)(2,1)} async-done(((bf16[512,512]{1,0:T(8,128)(2,1)}), bf16[512,512]{1,0:T(8,128)(2,1)}) %all-reduce.11.cloned.1.call-update) | async-done | bytes 524304 | tf_op jit(solution)/shard_map/psum | solution.py:64
  1262.7 1.8 fusion.48
  1264.6 5.5 convolution_bitcast_fusion.1
  (25 shorter events, 0.2 us)
Async XLA Ops:
  7.2 6.7 copy-start
  7.2 61.7 %all-reduce.5.cloned.1.call-start = ((), (), s32[]{:S(2)}) async-start(), calls=%async_computation | async-start | bytes 2097152 | tf_op jit(solution)/shard_map/psum | solution.py:39
  7.2 6.5 copy-start.6
  18.9 3.3 copy-start.2
  18.9 373.6 %all-reduce.9.cloned.1.call-start = ((), (), s32[]{:S(2)}) async-start(), calls=%async_computation.2 | async-start | bytes 9437184 | tf_op jit(solution)/shard_map/psum | solution.py:53
  28.4 40.4 %copy-start.5 = (f32[1,512]{1,0:T(1,128)S(1)}, f32[1,512]{1,0:T(1,128)}, u32[]{:S(2)}) copy-start(f32[1,512]{1,0:T(1,128)} %param.15) | copy-start | bytes 6148
  28.5 1032.5 %all-reduce.7.cloned.1.call-start = ((), (), s32[]{:S(2)}) async-start(), calls=%async_computation.1 | async-start | bytes 18874368 | tf_op jit(solution)/shard_map/psum | solution.py:58
  77.8 314.9 %copy-start.4 = (f32[4,2304]{1,0:T(4,128)S(1)}, f32[4,2304]{1,0:T(4,128)}, u32[]{:S(2)}) copy-start(f32[4,2304]{1,0:T(4,128)} %param.17) | copy-start | bytes 110596
  77.8 1133.0 %all-gather.2.cloned.1.call-start = ((), (), s32[]{:S(2)}) async-start(), calls=%async_computation.3 | async-start | bytes 23592960 | tf_op jit(solution)/shard_map/all_gather | solution.py:54
  392.5 870.3 %all-reduce.11.cloned.1.call-start = ((), (), s32[]{:S(2)}) async-start(), calls=%async_computation.4 | async-start | bytes 1048576 | tf_op jit(solution)/shard_map/psum | solution.py:64
  1220.9 7.3 copy-start.3
  1234.9 35.2 %copy-start.1 = (f32[1,1152,512]{2,1,0:T(8,128)S(1)}, f32[1,1152,512]{2,1,0:T(8,128)}, u32[]{:S(2)}) copy-start(f32[1,1152,512]{2,1,0:T(8,128)} %param.14) | copy-start | bytes 7077892
Sparse Core Ops, SparseCore 0:
  19.0 49.8 all-reduce.4
  72.1 320.3 all-reduce.8
  395.1 665.8 all-reduce.6
  1062.6 148.1 all-gather.1
  1228.3 34.3 all-reduce.10
where the time goes:
time: 1280 us
  waiting for transfers between devices  1190 us (93%)
  matrix products  42.9 us (3%)
  other arithmetic  18.5 us (1%)
  between operations  13.9 us (1%)
    psum x1, waiting for transfers between devices, shards(): summed_rows = lax.psum(recon_parts, ('layer', 'feat'))  668 us
    psum x1, waiting for transfers between devices, shards(): full_target = lax.psum(target_part, ('feat', 'par'))  315 us
    all_gather x1, waiting for transfers between devices, shards(): all_targets = lax.all_gather(full_target[None], 'layer', axis=0, tiled=True)  150 us
    psum x1, waiting for transfers between devices, shards(): pre_act = lax.psum(pre_part, 'par') + enc_bias[0]  40.3 us
  transfers between devices with their start and end apart: 5, of which 5 were waited for; matrix products, arithmetic and copies ran while one was open for 3% of the time, Pallas kernels for 0%

commit v1 on v0

v1 whole, which is shorter than its diff:
```python
import jax
import jax.numpy as jnp
from jax import lax
from jax.experimental import pallas as pl
from jax.experimental.pallas import tpu as pltpu
from jax.sharding import PartitionSpec as P

F32 = jnp.float32
BF16 = jnp.bfloat16
MESH = pl.DeviceIdType.MESH

T = 512
D = 2304
W = D // 2
F = 512
U = 288
Q1 = T // 4
Q2 = T // 16
CT = 384
RT = 256


def kernel(
    res_h, gain_v, gate_h, up_h, down_h, enc_h, ebias_v, dec_h, dbias_v,
    egrad_h, bgrad_v, dgrad_h,
    nrm, gate_v, up_v, down_v, hid, enc_v, enc_b, dec_v,
    pre_snd, pre_rcv, pos, act, act_t, acc,
    own, cs_snd, cs_rcv, r1_snd, r1_rcv, r2_snd, r2_rcv, x_snd, x_rcv, fin,
    err, back, bk_snd, bk_rcv, dpre, dg_v,
    ld_sem, out_sem, pre_s, pre_r, hd_s, hd_r, cs_s, cs_r, r1_s, r1_r, r2_s, r2_r, x_s, x_r,
    ga_s, ga_r, gb_s, gb_r, gc_s, gc_r, bk_s, bk_r,
):
    layer = lax.axis_index("layer")
    feat = lax.axis_index("feat")
    par = lax.axis_index("par")
    core = lax.rem(layer, 2)
    x_hi = lax.div(layer, 2)
    zz = lax.div(feat, 4)
    yy = lax.rem(feat, 4)
    a = zz + core * (yy - zz)
    b = yy + core * (zz - yy)
    home = core == par

    def at(first, second):
        return first * 4 + second + core * 3 * (second - first)

    par_id = (layer, feat, 1 - par)
    sib_id = (layer + 1 - 2 * core, feat, par)
    xhi_id = (lax.rem(layer + 2, 4), feat, par)
    step = [None] + [lax.rem(a + k, 4) for k in (1, 2, 3)]
    hop = [None] + [lax.rem(b + k, 4) for k in (1, 2, 3)]
    first_id = [None] + [(layer, at(step[k], b), par) for k in (1, 2, 3)]
    second_id = [None] + [(layer, at(a, hop[k]), par) for k in (1, 2, 3)]

    def remote(src, dst, s, r, to):
        return pltpu.make_async_remote_copy(
            src_ref=src, dst_ref=dst, send_sem=s, recv_sem=r, device_id=to, device_id_type=MESH
        )

    barrier = pltpu.get_barrier_semaphore()
    for to in [par_id, sib_id, xhi_id] + first_id[1:] + second_id[1:]:
        pl.semaphore_signal(barrier, inc=1, device_id=to, device_id_type=MESH)

    loads = [
        pltpu.make_async_copy(res_h.at[0], nrm, ld_sem.at[0]),
        pltpu.make_async_copy(enc_h.at[0], enc_v, ld_sem.at[1]),
        pltpu.make_async_copy(gate_h.at[0], gate_v, ld_sem.at[2]),
        pltpu.make_async_copy(up_h.at[0], up_v, ld_sem.at[3]),
        pltpu.make_async_copy(down_h.at[0], down_v.at[0], ld_sem.at[4]),
        pltpu.make_async_copy(dec_h.at[0, 0], dec_v, ld_sem.at[5]),
    ]
    for load in loads:
        load.start()

    loads[0].wait()

    def norm_rows(i, _):
        rows = pl.ds(pl.multiple_of(i * 32, 32), 32)
        x = nrm[rows, :].astype(F32)
        scale = lax.rsqrt(jnp.mean(x * x, axis=-1, keepdims=True) + 1e-6)
        nrm[rows, :] = (x * scale * gain_v[...]).astype(BF16)
        return 0

    lax.fori_loop(0, T // 32, norm_rows, 0)
    loads[1].wait()

    def enc_rows(i, _):
        rows = pl.ds(pl.multiple_of(i * 128, 128), 128)
        enc_b[rows, :] = enc_v[rows, :].astype(BF16)
        return 0

    lax.fori_loop(0, W // 128, enc_rows, 0)
    my_cols = pl.ds(pl.multiple_of(par * W, W), W)

    pl.semaphore_wait(barrier, 9)
    pre_copy = []
    for c in range(2):
        rows = pl.ds(c * RT, RT)
        part = jnp.dot(nrm[rows, my_cols], enc_b[...], preferred_element_type=F32)
        pos[rows, :] = part
        pre_snd[rows, :] = part.astype(BF16)
        pre_copy.append(remote(pre_snd.at[rows], pre_rcv.at[rows], pre_s.at[c], pre_r.at[c], par_id))
        pre_copy[c].start()

    loads[4].wait()
    down_copy = remote(down_v.at[0], down_v.at[1], hd_s.at[0], hd_r.at[0], par_id)
    hid_copy = remote(hid.at[0], hid.at[1], hd_s.at[1], hd_r.at[1], par_id)

    @pl.when(jnp.logical_not(home))
    def _():
        down_copy.start()

    loads[2].wait()
    loads[3].wait()

    def mlp_rows(i, _):
        rows = pl.ds(pl.multiple_of(i * RT, RT), RT)
        g = jnp.dot(nrm[rows, :], gate_v[...], preferred_element_type=F32)
        u = jnp.dot(nrm[rows, :], up_v[...], preferred_element_type=F32)
        inner = 0.7978845608028654 * (g + 0.044715 * g * g * g)
        hid[0, rows, :] = (0.5 * g * (1.0 + jnp.tanh(inner)) * u).astype(BF16)
        return 0

    lax.fori_loop(0, T // RT, mlp_rows, 0)

    @pl.when(jnp.logical_not(home))
    def _():
        hid_copy.start()

    for c in range(2):
        pre_copy[c].wait_recv()

        def act_rows(i, _):
            rows = pl.ds(pl.multiple_of(c * RT + i * 32, 32), 32)
            p = jnp.maximum(pos[rows, :] + pre_rcv[rows, :].astype(F32) + ebias_v[...], 0.0)
            pos[rows, :] = p
            act[rows, :] = (p * p).astype(BF16)
            return 0

        lax.fori_loop(0, RT // 32, act_rows, 0)
    loads[5].wait()

    slots = [1 - x_hi, x_hi]
    wave_copy = [None, None]

    def recon_tiles(k, half, r, to_sibling):
        j = slots[k]
        live = (2 * j + par >= layer).astype(F32)
        rows = pl.ds(r * RT, RT)

        def tile(n, _):
            local = pl.ds(pl.multiple_of(n * CT, CT), CT)
            cols = pl.ds(pl.multiple_of(half * W + n * CT, CT), CT)
            acc[...] = jnp.dot(act[rows, :], dec_v[j, :, cols], preferred_element_type=F32) * live
            if k == 1:

                @pl.when(home)
                def _():
                    acc[...] -= jnp.dot(
                        hid[0, rows, :], down_v[0, :, cols], preferred_element_type=F32
                    ) + jnp.dot(hid[1, rows, :], down_v[1, :, cols], preferred_element_type=F32)

            if to_sibling:
                cs_snd[k, rows, local] = acc[...].astype(BF16)
            else:
                own[k, rows, local] = acc[...]
            return 0

        lax.fori_loop(0, W // CT, tile, 0)

    def produce(k):
        copies = []
        for r in range(2):
            recon_tiles(k, 1 - core, r, True)
            rows = pl.ds(r * RT, RT)
            copies.append(
                remote(cs_snd.at[k, rows], cs_rcv.at[k, rows], cs_s.at[k, r], cs_r.at[k, r], sib_id)
            )
            copies[r].start()
        for r in range(2):
            recon_tiles(k, core, r, False)
        return copies

    def scatter_first(k, pair):
        for copy in pair:
            copy.wait_recv()
        copies = [None]
        for n in (1, 2, 3):

            def add_rows(i, _):
                rows = pl.ds(pl.multiple_of(step[n] * Q1 + i * 32, 32), 32)
                here = pl.ds(pl.multiple_of(i * 32, 32), 32)
                r1_snd[k, n - 1, here, :] = (own[k, rows, :] + cs_rcv[k, rows, :].astype(F32)).astype(BF16)
                return 0

            lax.fori_loop(0, Q1 // 32, add_rows, 0)
            copies.append(
                remote(r1_snd.at[k, n - 1], r1_rcv.at[k, n - 1], r1_s.at[k, n - 1], r1_r.at[k, n - 1], first_id[n])
            )
            copies[n].start()
        return copies

    def sum_first(k, q, _):
        rows = pl.ds(pl.multiple_of(a * Q1 + q * Q2, Q2), Q2)
        here = pl.ds(pl.multiple_of(q * Q2, Q2), Q2)
        total = own[k, rows, :] + cs_rcv[k, rows, :].astype(F32)
        for n in range(3):
            total = total + r1_rcv[k, n, here, :].astype(F32)
        return total

    def scatter_second(k, arrived):
        for n in (1, 2, 3):
            arrived[n].wait_recv()
        copies = [None]
        for n in (1, 2, 3):
            r2_snd[k, n - 1] = sum_first(k, hop[n], 0).astype(BF16)
            copies.append(
                remote(r2_snd.at[k, n - 1], r2_rcv.at[k, n - 1], r2_s.at[k, n - 1], r2_r.at[k, n - 1], second_id[n])
            )
            copies[n].start()
        fin[k] = sum_first(k, b, 0)
        return copies

    def finish(k, arrived):
        for n in (1, 2, 3):
            arrived[n].wait_recv()
        total = fin[k]
        for n in range(3):
            total = total + r2_rcv[k, n].astype(F32)
        fin[k] = total

    x_copy = remote(x_snd, x_rcv, x_s, x_r, xhi_id)

    def send_x(k):
        x_snd[...] = fin[k].astype(BF16)
        x_copy.start()

    low = x_hi == 0

    pair1 = [None]
    @pl.when(low)
    def _():
        pair = produce(0)
        scatter_first(0, pair)

    first0 = [None] + [
        remote(r1_snd.at[0, n - 1], r1_rcv.at[0, n - 1], r1_s.at[0, n - 1], r1_r.at[0, n - 1], first_id[n])
        for n in (1, 2, 3)
    ]

    act_t[...] = act[...].T

    @pl.when(home)
    def _():
        down_copy.wait_recv()
        hid_copy.wait_recv()

    pair1 = produce(1)

    @pl.when(low)
    def _():
        second = scatter_second(0, first0)

    first1 = scatter_first(1, pair1)

    @pl.when(low)
    def _():
        second = [None] + [
            remote(r2_snd.at[0, n - 1], r2_rcv.at[0, n - 1], r2_s.at[0, n - 1], r2_r.at[0, n - 1], second_id[n])
            for n in (1, 2, 3)
        ]
        finish(0, second)
        send_x(0)

    second1 = scatter_second(1, first1)
    finish(1, second1)

    @pl.when(jnp.logical_not(low))
    def _():
        send_x(1)

    half_cols = pl.ds(pl.multiple_of(core * W, W), W)
    my_rows = pl.ds(pl.multiple_of(a * Q1 + b * Q2, Q2), Q2)

    def write_error(j, total):
        bias = dbias_v[pl.ds(2 * j + par, 1), half_cols]
        err[core, j, my_rows, :] = ((total + bias) * 0.0625).astype(BF16)

    def gather_a(j, n):
        piece = err.at[core, j, my_rows]
        return remote(piece, piece, ga_s.at[j, n - 1], ga_r.at[j, n - 1], second_id[n])

    def block(first):
        return pl.ds(pl.multiple_of(first * Q1, Q1), Q1)

    def gather_b(j, n):
        piece = err.at[core, j, block(a)]
        return remote(piece, piece, gb_s.at[j, n - 1], gb_r.at[j, n - 1], first_id[n])

    def gather_c(j, n):
        piece = err.at[core, j, block(lax.rem(a + 4 - n, 4))]
        return remote(piece, piece, gc_s.at[j, n], gc_r.at[j, n], sib_id)

    def run_gather_a(j):
        for n in (1, 2, 3):
            gather_a(j, n).start()

    def run_gather_b(j):
        for n in (1, 2, 3):
            gather_a(j, n).wait_recv()
        for n in (1, 2, 3):
            gather_b(j, n).start()
        gather_c(j, 0).start()

    def run_gather_c(j):
        for n in (1, 2, 3):
            gather_b(j, n).wait_recv()
            gather_c(j, n).start()

    def wait_error(j):
        for n in range(4):
            rows = block(lax.rem(b + 4 - n, 4))
            remote(
                err.at[1 - core, j, rows], err.at[1 - core, j, rows], gc_s.at[j, n], gc_r.at[j, n], sib_id
            ).wait_recv()

    @pl.when(low)
    def _():
        write_error(0, fin[1])
        run_gather_a(0)

    x_copy.wait_recv()

    write_error(1, lax.select(jnp.broadcast_to(low, (Q2, W)), fin[0], fin[1]) + x_rcv[...].astype(F32))
    run_gather_a(1)

    @pl.when(low)
    def _():
        run_gather_b(0)

    run_gather_b(1)

    @pl.when(low)
    def _():
        run_gather_c(0)
        wait_error(0)

    live0 = par >= layer
    live1 = 2 + par >= layer

    def back_tile(j, r):
        rows = pl.ds(r * RT, RT)
        out = None
        for h in range(2):
            term = lax.dot_general(
                err[h, j, rows, :], dec_v[j, :, pl.ds(h * W, W)], (((1,), (1,)), ((), ())),
                preferred_element_type=F32,
            )
            out = term if out is None else out + term
        return out

    def dec_grad(j):
        def tile(n, _):
            for h in range(2):
                for m in range(2):
                    local = pl.ds(pl.multiple_of(n * CT, CT), CT)
                    cols = pl.ds(pl.multiple_of(h * W + n * CT, CT), CT)
                    rows = pl.ds(m * RT, RT)
                    dg_v[j, rows, cols] = jnp.dot(
                        act_t[rows, :], err[h, j, :, local], preferred_element_type=F32
                    ).astype(BF16)
            return 0

        lax.fori_loop(0, W // CT, tile, 0)

    def no_dec_grad(j):
        def rows_of(i, _):
            rows = pl.ds(pl.multiple_of(i * 32, 32), 32)
            dg_v[j, rows, :] = jnp.zeros((32, D), BF16)
            return 0

        lax.fori_loop(0, F // 32, rows_of, 0)

    outs = [pltpu.make_async_copy(dg_v.at[j], dgrad_h.at[0, 0, j], out_sem.at[j]) for j in range(2)]

    @pl.when(live0)
    def _():
        for r in range(2):
            back[pl.ds(r * RT, RT), :] = back_tile(0, r)
        dec_grad(0)

    @pl.when(jnp.logical_not(live0))
    def _():
        back[...] = jnp.zeros((T, F), F32)
        no_dec_grad(0)

    outs[0].start()
    run_gather_c(1)
    wait_error(1)

    bk_copy = []
    for r in range(2):
        rows = pl.ds(r * RT, RT)

        @pl.when(live1)
        def _():
            back[rows, :] += back_tile(1, r)

        bk_snd[rows, :] = back[rows, :].astype(BF16)
        bk_copy.append(remote(bk_snd.at[rows], bk_rcv.at[rows], bk_s.at[r], bk_r.at[r], par_id))
        bk_copy[r].start()

    @pl.when(live1)
    def _():
        dec_grad(1)

    @pl.when(jnp.logical_not(live1))
    def _():
        no_dec_grad(1)

    outs[1].start()

    bgrad_v[...] = jnp.zeros((1, F), F32)
    for r in range(2):
        bk_copy[r].wait_recv()

        def dpre_rows(i, _):
            rows = pl.ds(pl.multiple_of(r * RT + i * 32, 32), 32)
            d = (back[rows, :] + bk_rcv[rows, :].astype(F32)) * 2.0 * pos[rows, :]
            dpre[rows, :] = d.astype(BF16)
            bgrad_v[...] += jnp.sum(d, axis=0, keepdims=True)
            return 0

        lax.fori_loop(0, RT // 32, dpre_rows, 0)

    for n in range(W // CT):
        cols = pl.ds(pl.multiple_of(par * W + n * CT, 128), CT)
        enc_v[pl.ds(n * CT, CT), :] = lax.dot_general(
            nrm[:, cols], dpre[...], (((0,), (0,)), ((), ())), preferred_element_type=F32
        )
    last = pltpu.make_async_copy(enc_v, egrad_h.at[0], out_sem.at[2])
    last.start()

    for c in range(2):
        pre_copy[c].wait_send()
        bk_copy[c].wait_send()
        pair1[c].wait_send()

    @pl.when(jnp.logical_not(home))
    def _():
        down_copy.wait_send()
        hid_copy.wait_send()

    x_copy.wait_send()
    for n in (1, 2, 3):
        first1[n].wait_send()
        second1[n].wait_send()
        gather_a(1, n).wait_send()
        gather_b(1, n).wait_send()
    for n in range(4):
        gather_c(1, n).wait_send()

    @pl.when(low)
    def _():
        for r in range(2):
            rows = pl.ds(r * RT, RT)
            remote(cs_snd.at[0, rows], cs_rcv.at[0, rows], cs_s.at[0, r], cs_r.at[0, r], sib_id).wait_send()
        for n in (1, 2, 3):
            first0[n].wait_send()
            remote(
                r2_snd.at[0, n - 1], r2_rcv.at[0, n - 1], r2_s.at[0, n - 1], r2_r.at[0, n - 1], second_id[n]
            ).wait_send()
            gather_a(0, n).wait_send()
            gather_b(0, n).wait_send()
        for n in range(4):
            gather_c(0, n).wait_send()

    for copy in outs:
        copy.wait()
    last.wait()


def shards(
    residual, norm_gain, gate_weight, up_weight, down_weight, enc_weight, enc_bias, dec_weight, dec_bias
):
    any_spec = pl.BlockSpec(memory_space=pl.ANY)
    vmem = pl.BlockSpec(memory_space=pltpu.VMEM)
    dma = pltpu.SemaphoreType.DMA
    scratch = [
        pltpu.VMEM((T, D), BF16),
        pltpu.VMEM((D, U), BF16),
        pltpu.VMEM((D, U), BF16),
        pltpu.VMEM((2, U, D), BF16),
        pltpu.VMEM((2, T, U), BF16),
        pltpu.VMEM((W, F), F32),
        pltpu.VMEM((W, F), BF16),
        pltpu.VMEM((2, F, D), BF16),
        pltpu.VMEM((T, F), BF16),
        pltpu.VMEM((T, F), BF16),
        pltpu.VMEM((T, F), F32),
        pltpu.VMEM((T, F), BF16),
        pltpu.VMEM((F, T), BF16),
        pltpu.VMEM((RT, CT), F32),
        pltpu.VMEM((2, T, W), F32),
        pltpu.VMEM((2, T, W), BF16),
        pltpu.VMEM((2, T, W), BF16),
        pltpu.VMEM((2, 3, Q1, W), BF16),
        pltpu.VMEM((2, 3, Q1, W), BF16),
        pltpu.VMEM((2, 3, Q2, W), BF16),
        pltpu.VMEM((2, 3, Q2, W), BF16),
        pltpu.VMEM((Q2, W), BF16),
        pltpu.VMEM((Q2, W), BF16),
        pltpu.VMEM((2, Q2, W), F32),
        pltpu.VMEM((2, 2, T, W), BF16),
        pltpu.VMEM((T, F), F32),
        pltpu.VMEM((T, F), BF16),
        pltpu.VMEM((T, F), BF16),
        pltpu.VMEM((T, F), BF16),
        pltpu.VMEM((2, F, D), BF16),
        dma((6,)), dma((3,)),
        dma((2,)), dma((2,)),
        dma((2,)), dma((2,)),
        dma((2, 2)), dma((2, 2)),
        dma((2, 3)), dma((2, 3)),
        dma((2, 3)), dma((2, 3)),
        dma, dma,
        dma((2, 3)), dma((2, 3)),
        dma((2, 3)), dma((2, 3)),
        dma((2, 4)), dma((2, 4)),
        dma((2,)), dma((2,)),
    ]
    return pl.pallas_call(
        kernel,
        out_shape=(
            jax.ShapeDtypeStruct((1, W, F), F32),
            jax.ShapeDtypeStruct((1, F), F32),
            jax.ShapeDtypeStruct((1, 1, 2, F, D), BF16),
        ),
        in_specs=[any_spec, vmem, any_spec, any_spec, any_spec, any_spec, vmem, any_spec, vmem],
        out_specs=(any_spec, vmem, any_spec),
        scratch_shapes=scratch,
        compiler_params=pltpu.CompilerParams(
            collective_id=0, has_side_effects=True, vmem_limit_bytes=62 * 1024 * 1024
        ),
    )(residual, norm_gain, gate_weight, up_weight, down_weight, enc_weight, enc_bias, dec_weight, dec_bias)


def solution(mesh):
    return jax.shard_map(
        shards,
        mesh=mesh,
        in_specs=(
            P("layer", None, None),
            P("layer", None),
            P("layer", None, ("feat", "par")),
            P("layer", None, ("feat", "par")),
            P("layer", ("feat", "par"), None),
            P("layer", "par", "feat"),
            P("layer", "feat"),
            P("layer", "par", None, "feat", None),
            P(),
        ),
        out_specs=(
            P("layer", "par", "feat"),
            P("layer", "feat"),
            P("layer", "par", None, "feat", None),
        ),
        check_vma=False,
    )
```

time: 1280 us -> 117 us (0.09)
  waiting for transfers between devices: 1190 us -> 0 us
  Pallas kernels: 0 us -> 105 us
  matrix products: 42.9 us -> 0 us
  other arithmetic: 18.5 us -> 0 us
  between operations: 13.9 us -> 0.66 us
    psum x4 -> x0, waiting for transfers between devices: 1040 us -> none  [the longest x1 668 us: shards(): summed_rows = lax.psum(recon_parts, ('layer', 'feat'))]
    all_gather x1 -> x0, waiting for transfers between devices: 150 us -> none  [shards(): all_targets = lax.all_gather(full_target[None], 'layer', axis=0, tiled=True)]
    pallas_call x0 -> x1, Pallas kernels: none -> 105 us  [shards(): pl.pallas_call(kernel, out_shape=(jax.ShapeDtypeStruct((1, W, F), F32), j...]
    dot_general x7 -> x0, matrix products: 42.9 us -> none  [the longest x1 8.92 us: shards(): jnp.einsum('tf,jfd->jtd', actives, decoders, preferred_element_type=jnp.f...]
  transfers between devices with their start and end apart: 5 -> 0, of which waited for: 5 -> 0; matrix products, arithmetic and copies ran while one was open for 3% -> 0% of each run, Pallas kernels for 0% -> 0%
where the time goes in v1:
time: 117 us
  Pallas kernels  105 us (90%)
  local copies, waits for them, and re-layouts  11.3 us (10%)
    pallas_call x1, Pallas kernels, shards(): pl.pallas_call(kernel, out_shape=(jax.ShapeDtypeStruct((1, W, F), F32), j...  105 us
    unnamed x9, local copies, waits for them, and re-layouts  11.3 us

profile of v1, /device:TPU:1, one launch (start us, length us, event | category | flops | bytes accessed | tf_op | source)
XLA Modules:
  0.0 117.0 jit_solution(4638240912054140001)
XLA Ops:
  0.6 0.0 copy-start.1
  0.6 2.7 %copy.12.gate_h = bf16[1,2304,288]{2,1,0:T(8,128)(2,1)} copy(bf16[1,2304,288]{1,2,0:T(8,128)(2,1)} %param.11) | data formatting | bytes 2654208 | tf_op args[2]
  3.4 0.0 copy-done.1
  3.4 1.7 %copy.13.up_h = bf16[1,2304,288]{2,1,0:T(8,128)(2,1)} copy(bf16[1,2304,288]{1,2,0:T(8,128)(2,1)S(1)} %copy-done.1) | data formatting | bytes 2654208 | tf_op args[3]
  5.0 105.1 %shard_map.112 = (f32[1,1152,512]{2,1,0:T(8,128)}, f32[1,512]{1,0:T(1,128)}, bf16[1,1,2,512,2304]{4,3,2,1,0:T(8,128)(2,1)}) custom-call(bf16[1,512,2304]{2,1,0:T(8,128)(2,1)} %res_h.1, f32[1,2304]{1,0:T(1,128)} %gain_v.1, bf16[1,2304,288]{2,1,0:T(8,128)(2,1)} %copy.12.gate_h, bf16[1,2304,288]{2,1,0:T(8,128)(2,1)} %copy.13.up_h, ...), custom_call_target="tpu_custom_call" | custom-call | tf_op jit(solution)/shard_map/pallas_call | solution.py:532
  110.1 0.0 copy-start
  110.1 3.4 %copy.17 = f32[1,1152,512]{2,1,0:T(8,128)} copy(f32[1,1152,512]{2,1,0:T(8,128)} %get-tuple-element.6) | data formatting | bytes 4718592
  113.6 1.3 %copy.18 = f32[1,512]{1,0:T(1,128)} copy(f32[1,512]{1,0:T(1,128)} %get-tuple-element.7) | data formatting | bytes 4096
  114.8 0.0 copy-done
  114.8 2.2 %copy.19 = bf16[1,1,2,512,2304]{4,3,2,1,0:T(8,128)(2,1)} copy(bf16[1,1,2,512,2304]{4,3,2,1,0:T(8,128)(2,1)S(1)} %copy-done) | data formatting | bytes 9437184
Async XLA Ops:
  0.6 2.8 %copy-start.1 = (bf16[1,2304,288]{1,2,0:T(8,128)(2,1)S(1)}, bf16[1,2304,288]{1,2,0:T(8,128)(2,1)}, u32[]{:S(2)}) copy-start(bf16[1,2304,288]{1,2,0:T(8,128)(2,1)} %param.12) | copy-start | bytes 3981316
  110.1 4.7 %copy-start = (bf16[1,1,2,512,2304]{4,3,2,1,0:T(8,128)(2,1)S(1)}, bf16[1,1,2,512,2304]{4,3,2,1,0:T(8,128)(2,1)}, u32[]{:S(2)}) copy-start(bf16[1,1,2,512,2304]{4,3,2,1,0:T(8,128)(2,1)} %get-tuple-element.8) | copy-start | bytes 14155780

commit v2 on v0

v2 whole, which is shorter than its diff:
```python
import jax
import jax.numpy as jnp
from jax import lax
from jax.experimental import pallas as pl
from jax.experimental.pallas import tpu as pltpu
from jax.sharding import PartitionSpec as P

F32 = jnp.float32
BF16 = jnp.bfloat16
MESH = pl.DeviceIdType.MESH

T = 512
D = 2304
W = D // 2
F = 512
U = 288
Q1 = T // 4
QH = Q1 // 2
Q2 = T // 16
CT = 384
RT = 256
BT = 128


def kernel(
    res_h, gain_v, gate_h, up_h, down_h, enc_h, ebias_v, dec_h, dbias_v,
    rows_h, dpre_h, bgrad_v, dgrad_h,
    nrm, rows_t, gate_v, up_v, down_v, hid, enc_v, enc_b, dec_v,
    pre_snd, pre_rcv, pos, act, act_t,
    own, cs_snd, cs_rcv, part, relay, r1_rcv, r2_snd, r2_rcv, fin, tg_snd, tg_rcv, x_snd, x_rcv,
    err, back, bk_snd, bk_rcv, dpre, dg_v,
    ld_sem, out_sem, pre_s, pre_r, cs_s, cs_r, r1_s, r1_r, r2_s, r2_r, tg_s, tg_r, x_s, x_r,
    ga_s, ga_r, gb_s, gb_r, gc_s, gc_r, bk_s, bk_r,
):
    layer = lax.axis_index("layer")
    feat = lax.axis_index("feat")
    par = lax.axis_index("par")
    core = lax.rem(layer, 2)
    x_hi = lax.div(layer, 2)
    zz = lax.div(feat, 4)
    yy = lax.rem(feat, 4)
    low = x_hi == 0
    home = core == par
    away = core != par

    def first_of(role):
        return zz + role * (yy - zz)

    def second_of(role):
        return yy + role * (zz - yy)

    def at(role, first, second):
        return (layer, first * 4 + second + role * 3 * (second - first), par)

    def turn(x, n):
        return lax.rem(x + n, 4)

    sib = layer + 1 - 2 * core
    par_id = (layer, feat, 1 - par)
    sib_id = (sib, feat, par)
    diag_id = (sib, feat, 1 - par)
    xhi_id = (turn(layer, 2), feat, par)

    def remote(src, dst, s, r, to):
        return pltpu.make_async_remote_copy(
            src_ref=src, dst_ref=dst, send_sem=s, recv_sem=r, device_id=to, device_id_type=MESH
        )

    barrier = pltpu.get_barrier_semaphore()
    peers = [par_id, sib_id, diag_id, xhi_id]
    for n in (1, 2, 3):
        peers += [at(0, turn(zz, n), yy), at(0, zz, turn(yy, n))]
    for to in peers:
        pl.semaphore_signal(barrier, inc=1, device_id=to, device_id_type=MESH)

    loads = [
        pltpu.make_async_copy(res_h.at[0], nrm, ld_sem.at[0]),
        pltpu.make_async_copy(enc_h.at[0], enc_v, ld_sem.at[1]),
        pltpu.make_async_copy(gate_h.at[0], gate_v, ld_sem.at[2]),
        pltpu.make_async_copy(up_h.at[0], up_v, ld_sem.at[3]),
        pltpu.make_async_copy(down_h.at[0], down_v, ld_sem.at[4]),
        pltpu.make_async_copy(dec_h.at[0, 0], dec_v, ld_sem.at[5]),
    ]
    for load in loads:
        load.start()

    def loop(count, size, body):
        def run(i, _):
            body(pl.ds(pl.multiple_of(i * size, size), size))
            return 0

        lax.fori_loop(0, count // size, run, 0)

    loads[0].wait()

    def norm_rows(rows):
        x = nrm[rows, :].astype(F32)
        scale = lax.rsqrt(jnp.mean(x * x, axis=-1, keepdims=True) + 1e-6)
        nrm[rows, :] = (x * scale * gain_v[...]).astype(BF16)

    loop(T, 32, norm_rows)
    loads[1].wait()

    def enc_rows(rows):
        enc_b[rows, :] = enc_v[rows, :].astype(BF16)

    loop(W, 128, enc_rows)
    my_cols = pl.ds(pl.multiple_of(par * W, W), W)
    rows_copy = pltpu.make_async_copy(rows_t, rows_h, out_sem.at[2])

    pl.semaphore_wait(barrier, len(peers))
    pre_copy = []
    for c in range(2):
        rows = pl.ds(c * RT, RT)
        partial = jnp.dot(nrm[rows, my_cols], enc_b[...], preferred_element_type=F32)
        pos[rows, :] = partial
        pre_snd[rows, :] = partial.astype(BF16)
        pre_copy.append(remote(pre_snd.at[rows], pre_rcv.at[rows], pre_s.at[c], pre_r.at[c], par_id))
        pre_copy[c].start()

    loads[2].wait()
    loads[3].wait()

    def mlp_rows(rows):
        x = nrm[rows, :]
        g = lax.dot_general(x, gate_v[...], (((1,), (1,)), ((), ())), preferred_element_type=F32)
        u = lax.dot_general(x, up_v[...], (((1,), (1,)), ((), ())), preferred_element_type=F32)
        inner = 0.7978845608028654 * (g + 0.044715 * g * g * g)
        hid[rows, :] = (0.5 * g * (1.0 + jnp.tanh(inner)) * u).astype(BF16)

    loop(T, RT, mlp_rows)
    loads[4].wait()

    def role_of(u):
        return u if u < 2 else core

    def half_rows(blk, half):
        return pl.ds(pl.multiple_of(blk * Q1 + half * QH, QH), QH)

    def ring(u, m):
        role = role_of(u)
        i, k = first_of(role), second_of(role)
        up1, down1, far = turn(i, 1), turn(i, 3), turn(i, 2)
        right, left = at(role, up1, k), at(role, down1, k)
        src, to = [
            (lambda: part.at[u, half_rows(far, 0)], right),
            (lambda: part.at[u, half_rows(far, 1)], left),
            (lambda: part.at[u, half_rows(up1, 1)], right),
            (lambda: part.at[u, half_rows(down1, 0)], left),
            (lambda: relay.at[u, 0], right),
            (lambda: relay.at[u, 1], left),
        ][m]
        return remote(src(), r1_rcv.at[u, m], r1_s.at[u, m], r1_r.at[u, m], to)

    def ring_start(u):
        for m in range(4):
            ring(u, m).start()

    def ring_relay(u):
        i = first_of(role_of(u))
        for m, blk in ((0, turn(i, 1)), (1, turn(i, 3))):
            ring(u, m).wait_recv()
            relay[u, m] = (r1_rcv[u, m].astype(F32) + part[u, half_rows(blk, m), :].astype(F32)).astype(BF16)
            ring(u, 4 + m).start()

    def second_copy(u, n):
        role = role_of(u)
        to = at(role, first_of(role), turn(second_of(role), n))
        return remote(r2_snd.at[u, n - 1], r2_rcv.at[u, n - 1], r2_s.at[u, n - 1], r2_r.at[u, n - 1], to)

    def second_start(u):
        role = role_of(u)
        i, k = first_of(role), second_of(role)
        for m in (2, 3, 4, 5):
            ring(u, m).wait_recv()

        def piece(q):
            half = lax.div(q, 2)
            here = pl.ds(pl.multiple_of(lax.rem(q, 2) * Q2, Q2), Q2)
            rows = pl.ds(pl.multiple_of(i * Q1 + q * Q2, Q2), Q2)
            return (
                part[u, rows, :].astype(F32)
                + r1_rcv[u, 3 - half, here, :].astype(F32)
                + r1_rcv[u, 4 + half, here, :].astype(F32)
            )

        for n in (1, 2, 3):
            r2_snd[u, n - 1] = piece(turn(k, n)).astype(BF16)
            second_copy(u, n).start()
        fin[u] = piece(k)

    def second_end(u):
        for n in (1, 2, 3):
            second_copy(u, n).wait_recv()
        total = fin[u]
        for n in range(3):
            total = total + r2_rcv[u, n].astype(F32)
        fin[u] = total

    for h in range(2):

        def down_cols(local):
            cols = pl.ds(pl.multiple_of(local.start + h * W, CT), CT)
            part[h, :, local] = jnp.dot(hid[...], down_v[:, cols], preferred_element_type=F32).astype(BF16)

        loop(W, CT, down_cols)

        @pl.when(away)
        def _():
            ring_start(h)

    live0 = par >= layer
    live1 = 2 + par >= layer
    half_cols = pl.ds(pl.multiple_of(core * W, W), W)

    def activate(c):
        pre_copy[c].wait_recv()

        def act_rows(rows):
            rows = pl.ds(pl.multiple_of(c * RT + rows.start, 32), 32)
            p = jnp.maximum(pos[rows, :] + pre_rcv[rows, :].astype(F32) + ebias_v[...], 0.0)
            pos[rows, :] = p
            act[rows, :] = (p * p).astype(BF16)

        loop(RT, 32, act_rows)

    def core_copy(j, r):
        rows = pl.ds(r * RT, RT)
        return remote(cs_snd.at[j, rows], cs_rcv.at[j, rows], cs_s.at[j, r], cs_r.at[j, r], sib_id)

    def recon(j, r):
        live = (live1 if j == 1 else live0).astype(F32)
        ours = jnp.logical_and(home, x_hi == j).astype(F32)
        rows = pl.ds(r * RT, RT)
        x = act[rows, :]

        def tile(half, local):
            cols = pl.ds(pl.multiple_of(half * W + local.start, CT), CT)
            out = jnp.dot(x, dec_v[j, :, cols], preferred_element_type=F32)
            return out * live - part[half, rows, local].astype(F32) * ours

        def for_sibling(local):
            cs_snd[j, rows, local] = tile(1 - core, local).astype(BF16)

        def for_self(local):
            own[j, rows, local] = tile(core, local)

        loop(W, CT, for_sibling)
        core_copy(j, r).start()
        loop(W, CT, for_self)

    def chip_sum(j):
        for r in range(2):
            core_copy(j, r).wait_recv()

        def add_rows(rows):
            part[3 - j, rows, :] = (own[j, rows, :] + cs_rcv[j, rows, :].astype(F32)).astype(BF16)

        loop(T, 32, add_rows)

    tg_par = remote(tg_snd.at[0], tg_rcv, tg_s.at[0], tg_r, par_id)
    tg_diag = remote(tg_snd.at[1], tg_rcv, tg_s.at[1], tg_r, diag_id)

    activate(0)
    loads[5].wait()
    recon(1, 0)

    @pl.when(away)
    def _():
        ring_relay(0)
        ring_relay(1)

    activate(1)
    recon(1, 1)

    @pl.when(low)
    def _():
        recon(0, 0)

    chip_sum(1)
    ring_start(2)

    @pl.when(away)
    def _():
        second_start(0)
        second_start(1)

    @pl.when(low)
    def _():
        recon(0, 1)

    ring_relay(2)

    @pl.when(low)
    def _():
        chip_sum(0)
        ring_start(3)

    @pl.when(away)
    def _():
        second_end(0)
        second_end(1)
        tg_snd[0] = fin[core].astype(BF16)
        tg_snd[1] = fin[1 - core].astype(BF16)
        tg_par.start()
        tg_diag.start()

    second_start(2)

    @pl.when(low)
    def _():
        ring_relay(3)

    second_end(2)
    x_copy = remote(x_snd, x_rcv, x_s, x_r, xhi_id)
    a, b = first_of(core), second_of(core)
    my_rows = pl.ds(pl.multiple_of(a * Q1 + b * Q2, Q2), Q2)

    def write_error(j, total):
        bias = dbias_v[pl.ds(2 * j + par, 1), half_cols]
        err[core, j, my_rows, :] = ((total + bias) * 0.0625).astype(BF16)

    def take_target(u):
        tg_par.wait_recv()
        fin[u] = fin[u] - tg_rcv[...].astype(F32)

    @pl.when(jnp.logical_not(low))
    def _():
        take_target(2)

    x_snd[...] = fin[2].astype(BF16)
    x_copy.start()
    act_t[...] = act[...].T
    for n in range(W // CT):
        cols = pl.ds(pl.multiple_of(par * W + n * CT, 128), CT)
        rows_t[pl.ds(n * CT, CT), :] = nrm[:, cols].T
    rows_copy.start()

    @pl.when(low)
    def _():
        second_start(3)

    def block(first):
        return pl.ds(pl.multiple_of(first * Q1, Q1), Q1)

    def gather_a(j, n):
        piece = err.at[core, j, my_rows]
        return remote(piece, piece, ga_s.at[j, n - 1], ga_r.at[j, n - 1], at(core, a, turn(b, n)))

    def gather_b(j, m):
        rows, n = [
            (block(a), 1), (block(a), 3), (half_rows(turn(a, 3), 0), 1), (half_rows(turn(a, 1), 1), 3)
        ][m]
        piece = err.at[core, j, rows]
        return remote(piece, piece, gb_s.at[j, m], gb_r.at[j, m], at(core, turn(a, n), b))

    def gather_c(j, n):
        piece = err.at[core, j, block(turn(a, n))]
        return remote(piece, piece, gc_s.at[j, n], gc_r.at[j, n], sib_id)

    def gather_1(j):
        for n in (1, 2, 3):
            gather_a(j, n).start()

    def gather_2(j):
        for n in (1, 2, 3):
            gather_a(j, n).wait_recv()
        gather_b(j, 0).start()
        gather_b(j, 1).start()
        gather_c(j, 0).start()

    def gather_3(j):
        gather_b(j, 0).wait_recv()
        gather_b(j, 2).start()
        gather_c(j, 3).start()
        gather_b(j, 1).wait_recv()
        gather_b(j, 3).start()
        gather_c(j, 1).start()

    def gather_4(j):
        gather_b(j, 2).wait_recv()
        gather_b(j, 3).wait_recv()
        gather_c(j, 2).start()

    def wait_error(j):
        for n in range(4):
            gather_c(j, n).wait_recv()

    def back_tile(j, rows):
        out = None
        for h in range(2):
            term = lax.dot_general(
                err[h, j, rows, :], dec_v[j, :, pl.ds(h * W, W)], (((1,), (1,)), ((), ())),
                preferred_element_type=F32,
            )
            out = term if out is None else out + term
        return out

    def dec_grad(j):
        for h in range(2):

            def grad_cols(local):
                cols = pl.ds(pl.multiple_of(local.start + h * W, CT), CT)
                dg_v[j, :, cols] = jnp.dot(
                    act_t[...], err[h, j, :, local], preferred_element_type=F32
                ).astype(BF16)

            loop(W, CT, grad_cols)

    def no_dec_grad(j):
        def zero_rows(rows):
            dg_v[j, rows, :] = jnp.zeros((32, D), BF16)

        loop(F, 32, zero_rows)

    outs = [pltpu.make_async_copy(dg_v.at[j], dgrad_h.at[j], out_sem.at[j]) for j in range(2)]

    x_copy.wait_recv()
    write_error(1, fin[2] + x_rcv[...].astype(F32))
    gather_1(1)

    @pl.when(low)
    def _():
        second_end(3)
        take_target(3)
        write_error(0, fin[3])
        gather_1(0)

    gather_2(1)

    @pl.when(low)
    def _():
        gather_2(0)

    gather_3(1)

    @pl.when(low)
    def _():
        gather_3(0)

    gather_4(1)
    wait_error(1)

    def back_first(r):
        rows = pl.ds(r * RT, RT)

        @pl.when(live1)
        def _():
            back[rows, :] = back_tile(1, rows)

        @pl.when(jnp.logical_not(live1))
        def _():
            back[rows, :] = jnp.zeros((RT, F), F32)

    back_first(0)

    @pl.when(low)
    def _():
        gather_4(0)

    back_first(1)

    @pl.when(low)
    def _():
        wait_error(0)

    bk_copy = []
    for r in range(T // BT):
        rows = pl.ds(r * BT, BT)

        @pl.when(live0)
        def _():
            back[rows, :] += back_tile(0, rows)

        bk_snd[rows, :] = back[rows, :].astype(BF16)
        bk_copy.append(remote(bk_snd.at[rows], bk_rcv.at[rows], bk_s.at[r], bk_r.at[r], par_id))
        bk_copy[r].start()

    for j, live in ((1, live1), (0, live0)):

        @pl.when(live)
        def _():
            dec_grad(j)

        @pl.when(jnp.logical_not(live))
        def _():
            no_dec_grad(j)

        outs[j].start()

    bgrad_v[...] = jnp.zeros((1, F), F32)
    for r in range(T // BT):
        bk_copy[r].wait_recv()

        def dpre_rows(rows):
            rows = pl.ds(pl.multiple_of(r * BT + rows.start, 32), 32)
            d = (back[rows, :] + bk_rcv[rows, :].astype(F32)) * 2.0 * pos[rows, :]
            dpre[rows, :] = d.astype(BF16)
            bgrad_v[...] += jnp.sum(d, axis=0, keepdims=True)

        loop(BT, 32, dpre_rows)

    last = pltpu.make_async_copy(dpre, dpre_h, out_sem.at[3])
    last.start()

    for copy in pre_copy + bk_copy:
        copy.wait_send()

    def drain(u, j):
        for m in range(6):
            ring(u, m).wait_send()
        for n in (1, 2, 3):
            second_copy(u, n).wait_send()
        if j is not None:
            for r in range(2):
                core_copy(j, r).wait_send()
            for n in (1, 2, 3):
                gather_a(j, n).wait_send()
            for n in range(4):
                gather_b(j, n).wait_send()
                gather_c(j, n).wait_send()

    drain(2, 1)

    @pl.when(low)
    def _():
        drain(3, 0)

    @pl.when(away)
    def _():
        drain(0, None)
        drain(1, None)
        tg_par.wait_send()
        tg_diag.wait_send()

    x_copy.wait_send()
    for copy in outs:
        copy.wait()
    rows_copy.wait()
    last.wait()


def finish_kernel(
    rows_h, dpre_h, bsum_v, dgrad_h, egrad_h, bgrad_v, dout_h, rows_v, dpre_v, eg_v, dg_v, ld_sem, in_sem, out_sem, cp_sem
):
    loads = [
        pltpu.make_async_copy(dpre_h, dpre_v, ld_sem.at[0]),
        pltpu.make_async_copy(rows_h, rows_v, ld_sem.at[1]),
    ]
    here = [(j, pl.ds(r * RT, RT)) for j in range(2) for r in range(2)]
    arrive = [pltpu.make_async_copy(dgrad_h.at[p], dg_v.at[p], in_sem.at[n]) for n, p in enumerate(here)]
    leave = [pltpu.make_async_copy(dg_v.at[p], dout_h.at[(0, 0) + p], cp_sem.at[n]) for n, p in enumerate(here)]
    for copy in loads + arrive:
        copy.start()
    for copy in loads:
        copy.wait()
    bgrad_v[...] = bsum_v[...]
    outs = []
    for n in range(W // CT):
        rows = pl.ds(n * CT, CT)
        eg_v[rows, :] = jnp.dot(rows_v[rows, :], dpre_v[...], preferred_element_type=F32)
        outs.append(pltpu.make_async_copy(eg_v.at[rows], egrad_h.at[0, rows], out_sem.at[n]))
        outs[n].start()
        arrive[n].wait()
        leave[n].start()
    arrive[3].wait()
    leave[3].start()
    for copy in outs + leave:
        copy.wait()


def shards(
    residual, norm_gain, gate_weight, up_weight, down_weight, enc_weight, enc_bias, dec_weight, dec_bias
):
    any_spec = pl.BlockSpec(memory_space=pl.ANY)
    vmem = pl.BlockSpec(memory_space=pltpu.VMEM)
    dma = pltpu.SemaphoreType.DMA

    def pair(*shape):
        return [dma(shape), dma(shape)]

    scratch = [
        pltpu.VMEM((T, D), BF16),
        pltpu.VMEM((W, T), BF16),
        pltpu.VMEM((U, D), BF16),
        pltpu.VMEM((U, D), BF16),
        pltpu.VMEM((U, D), BF16),
        pltpu.VMEM((T, U), BF16),
        pltpu.VMEM((W, F), F32),
        pltpu.VMEM((W, F), BF16),
        pltpu.VMEM((2, F, D), BF16),
        pltpu.VMEM((T, F), BF16),
        pltpu.VMEM((T, F), BF16),
        pltpu.VMEM((T, F), F32),
        pltpu.VMEM((T, F), BF16),
        pltpu.VMEM((F, T), BF16),
        pltpu.VMEM((2, T, W), F32),
        pltpu.VMEM((2, T, W), BF16),
        pltpu.VMEM((2, T, W), BF16),
        pltpu.VMEM((4, T, W), BF16),
        pltpu.VMEM((4, 2, QH, W), BF16),
        pltpu.VMEM((4, 6, QH, W), BF16),
        pltpu.VMEM((4, 3, Q2, W), BF16),
        pltpu.VMEM((4, 3, Q2, W), BF16),
        pltpu.VMEM((4, Q2, W), F32),
        pltpu.VMEM((2, Q2, W), BF16),
        pltpu.VMEM((Q2, W), BF16),
        pltpu.VMEM((Q2, W), BF16),
        pltpu.VMEM((Q2, W), BF16),
        pltpu.VMEM((2, 2, T, W), BF16),
        pltpu.VMEM((T, F), F32),
        pltpu.VMEM((T, F), BF16),
        pltpu.VMEM((T, F), BF16),
        pltpu.VMEM((T, F), BF16),
        pltpu.VMEM((2, F, D), BF16),
        dma((6,)), dma((4,)),
    ]
    scratch += pair(2) + pair(2, 2) + pair(4, 6) + pair(4, 3)
    scratch += [dma((2,)), dma, dma, dma]
    scratch += pair(2, 3) + pair(2, 4) + pair(2, 4) + pair(T // BT)
    rows, dpre, bsum, dgrad = pl.pallas_call(
        kernel,
        out_shape=(
            jax.ShapeDtypeStruct((W, T), BF16),
            jax.ShapeDtypeStruct((T, F), BF16),
            jax.ShapeDtypeStruct((1, F), F32),
            jax.ShapeDtypeStruct((2, F, D), BF16),
        ),
        in_specs=[any_spec, vmem, any_spec, any_spec, any_spec, any_spec, vmem, any_spec, vmem],
        out_specs=(any_spec, any_spec, vmem, any_spec),
        scratch_shapes=scratch,
        compiler_params=pltpu.CompilerParams(
            collective_id=0, has_side_effects=True, vmem_limit_bytes=62 * 1024 * 1024
        ),
    )(
        residual,
        norm_gain,
        jnp.swapaxes(gate_weight, 1, 2),
        jnp.swapaxes(up_weight, 1, 2),
        down_weight,
        enc_weight,
        enc_bias,
        dec_weight,
        dec_bias,
    )
    return pl.pallas_call(
        finish_kernel,
        out_shape=(
            jax.ShapeDtypeStruct((1, W, F), F32),
            jax.ShapeDtypeStruct((1, F), F32),
            jax.ShapeDtypeStruct((1, 1, 2, F, D), BF16),
        ),
        in_specs=[any_spec, any_spec, vmem, any_spec],
        out_specs=(any_spec, vmem, any_spec),
        scratch_shapes=[
            pltpu.VMEM((W, T), BF16),
            pltpu.VMEM((T, F), BF16),
            pltpu.VMEM((W, F), F32),
            pltpu.VMEM((2, F, D), BF16),
            dma((2,)),
            dma((4,)),
            dma((W // CT,)),
            dma((4,)),
        ],
        compiler_params=pltpu.CompilerParams(vmem_limit_bytes=62 * 1024 * 1024),
    )(rows, dpre, bsum, dgrad)


def solution(mesh):
    return jax.shard_map(
        shards,
        mesh=mesh,
        in_specs=(
            P("layer", None, None),
            P("layer", None),
            P("layer", None, ("feat", "par")),
            P("layer", None, ("feat", "par")),
            P("layer", ("feat", "par"), None),
            P("layer", "par", "feat"),
            P("layer", "feat"),
            P("layer", "par", None, "feat", None),
            P(),
        ),
        out_specs=(
            P("layer", "par", "feat"),
            P("layer", "feat"),
            P("layer", "par", None, "feat", None),
        ),
        check_vma=False,
    )
```

time: 1280 us -> 94.7 us (0.07)
  waiting for transfers between devices: 1190 us -> 0 us
  Pallas kernels: 0 us -> 93.9 us
  matrix products: 42.9 us -> 0 us
  other arithmetic: 18.5 us -> 0 us
  between operations: 13.9 us -> 0.64 us
    psum x4 -> x0, waiting for transfers between devices: 1040 us -> none  [the longest x1 668 us: shards(): summed_rows = lax.psum(recon_parts, ('layer', 'feat'))]
    all_gather x1 -> x0, waiting for transfers between devices: 150 us -> none  [shards(): all_targets = lax.all_gather(full_target[None], 'layer', axis=0, tiled=True)]
    pallas_call x0 -> x2, Pallas kernels: none -> 93.9 us  [the longest x1 86.7 us: shards(): pl.pallas_call(kernel, out_shape=(jax.ShapeDtypeStruct((W, T), BF16), jax...]
    dot_general x7 -> x0, matrix products: 42.9 us -> none  [the longest x1 8.92 us: shards(): jnp.einsum('tf,jfd->jtd', actives, decoders, preferred_element_type=jnp.f...]
  transfers between devices with their start and end apart: 5 -> 0, of which waited for: 5 -> 0; matrix products, arithmetic and copies ran while one was open for 3% -> 0% of each run, Pallas kernels for 0% -> 0%
where the time goes in v2:
time: 94.7 us; the launch traced here: 94.5 us
  Pallas kernels  93.9 us (99%)
    pallas_call x1, Pallas kernels, shards(): pl.pallas_call(kernel, out_shape=(jax.ShapeDtypeStruct((W, T), BF16), jax...  86.7 us
    pallas_call x1, Pallas kernels, shards(): pl.pallas_call(finish_kernel, out_shape=(jax.ShapeDtypeStruct((1, W, F),...  7.15 us

profile of v2, /device:TPU:1, one launch (start us, length us, event | category | flops | bytes accessed | tf_op | source)
XLA Modules:
  0.0 94.5 jit_solution(14549482460150731521)
XLA Ops:
  0.6 86.7 %shard_map.112 = (bf16[1152,512]{1,0:T(8,128)(2,1)}, bf16[512,512]{1,0:T(8,128)(2,1)}, f32[1,512]{1,0:T(1,128)}, bf16[2,512,2304]{2,1,0:T(8,128)(2,1)}) custom-call(bf16[1,512,2304]{2,1,0:T(8,128)(2,1)} %res_h.1, f32[1,2304]{1,0:T(1,128)} %gain_v.1, bf16[1,288,2304]{2,1,0:T(8,128)(2,1)} %bitcast.2, bf16[1,288,2304]{2,1,0:T(8,128)(2,1)} %bitcast.3, ...), custom_call_target="tpu_custom_call" | custom-call | tf_op jit(solution)/shard_map/pallas_call | solution.py:621
  87.4 7.2 %shard_map.113 = (f32[1,1152,512]{2,1,0:T(8,128)}, f32[1,512]{1,0:T(1,128)}, bf16[1,1,2,512,2304]{4,3,2,1,0:T(8,128)(2,1)}) custom-call(bf16[1152,512]{1,0:T(8,128)(2,1)} %get-tuple-element.7.rows_h, bf16[512,512]{1,0:T(8,128)(2,1)} %get-tuple-element.8.dpre_h, f32[1,512]{1,0:T(1,128)} %get-tuple-element.9.bsum_v, ...), custom_call_target="tpu_custom_call" | custom-call | tf_op jit(solution)/shard_map/pallas_call | solution.py:646

commit v3 on v2

--- a/solution.py
+++ b/solution.py
@@ -14,11 +14,11 @@
 W = D // 2
 F = 512
 U = 288
-Q1 = T // 4
+RT = 256
+Q1 = RT // 4
 QH = Q1 // 2
-Q2 = T // 16
+Q2 = RT // 16
 CT = 384
-RT = 256
 BT = 128
 
 
@@ -128,11 +128,24 @@
         inner = 0.7978845608028654 * (g + 0.044715 * g * g * g)
         hid[rows, :] = (0.5 * g * (1.0 + jnp.tanh(inner)) * u).astype(BF16)
 
-    loop(T, RT, mlp_rows)
-    loads[4].wait()
+    def mlp(t):
+        mlp_rows(pl.ds(t * RT, RT))
+        for h in range(2):
+
+            def down_cols(local):
+                cols = pl.ds(pl.multiple_of(local.start + h * W, CT), CT)
+                part[2 * t + h, :, local] = jnp.dot(
+                    hid[t * RT : (t + 1) * RT, :], down_v[:, cols], preferred_element_type=F32
+                ).astype(BF16)
+
+            loop(W, CT, down_cols)
+
+            @pl.when(away)
+            def _():
+                ring_start(2 * t + h)
 
     def role_of(u):
-        return u if u < 2 else core
+        return u % 2 if u < 4 else core
 
     def half_rows(blk, half):
         return pl.ds(pl.multiple_of(blk * Q1 + half * QH, QH), QH)
@@ -197,18 +210,6 @@
             total = total + r2_rcv[u, n].astype(F32)
         fin[u] = total
 
-    for h in range(2):
-
-        def down_cols(local):
-            cols = pl.ds(pl.multiple_of(local.start + h * W, CT), CT)
-            part[h, :, local] = jnp.dot(hid[...], down_v[:, cols], preferred_element_type=F32).astype(BF16)
-
-        loop(W, CT, down_cols)
-
-        @pl.when(away)
-        def _():
-            ring_start(h)
-
     live0 = par >= layer
     live1 = 2 + par >= layer
     half_cols = pl.ds(pl.multiple_of(core * W, W), W)
@@ -237,7 +238,7 @@
         def tile(half, local):
             cols = pl.ds(pl.multiple_of(half * W + local.start, CT), CT)
             out = jnp.dot(x, dec_v[j, :, cols], preferred_element_type=F32)
-            return out * live - part[half, rows, local].astype(F32) * ours
+            return out * live - part[2 * r + half, :, local].astype(F32) * ours
 
         def for_sibling(local):
             cs_snd[j, rows, local] = tile(1 - core, local).astype(BF16)
@@ -249,142 +250,183 @@
         core_copy(j, r).start()
         loop(W, CT, for_self)
 
-    def chip_sum(j):
-        for r in range(2):
-            core_copy(j, r).wait_recv()
+    def chip_sum(j, t):
+        core_copy(j, t).wait_recv()
 
         def add_rows(rows):
-            part[3 - j, rows, :] = (own[j, rows, :] + cs_rcv[j, rows, :].astype(F32)).astype(BF16)
-
-        loop(T, 32, add_rows)
-
-    tg_par = remote(tg_snd.at[0], tg_rcv, tg_s.at[0], tg_r, par_id)
-    tg_diag = remote(tg_snd.at[1], tg_rcv, tg_s.at[1], tg_r, diag_id)
-
+            whole = pl.ds(pl.multiple_of(t * RT + rows.start, 32), 32)
+            part[unit(j, t), rows, :] = (own[j, whole, :] + cs_rcv[j, whole, :].astype(F32)).astype(BF16)
+
+        loop(RT, 32, add_rows)
+        ring_start(unit(j, t))
+
+    def unit(j, t):
+        return 5 + 2 * t - j
+
+    def tg_par(t):
+        return remote(tg_snd.at[t, 0], tg_rcv.at[t], tg_s.at[t, 0], tg_r.at[t], par_id)
+
+    def tg_diag(t):
+        return remote(tg_snd.at[t, 1], tg_rcv.at[t], tg_s.at[t, 1], tg_r.at[t], diag_id)
+
+    def x_copy(t):
+        return remote(x_snd.at[t], x_rcv.at[t], x_s.at[t], x_r.at[t], xhi_id)
+
+    a, b = first_of(core), second_of(core)
+
+    def piece_rows(t):
+        return pl.ds(pl.multiple_of(t * RT + a * Q1 + b * Q2, Q2), Q2)
+
+    def write_error(j, t, total):
+        bias = dbias_v[pl.ds(2 * j + par, 1), half_cols]
+        err[core, j, piece_rows(t), :] = ((total + bias) * 0.0625).astype(BF16)
+
+    def take_target(j, t):
+        tg_par(t).wait_recv()
+        fin[unit(j, t)] = fin[unit(j, t)] - tg_rcv[t].astype(F32)
+
+    def block(t, first):
+        return pl.ds(pl.multiple_of(t * RT + first * Q1, Q1), Q1)
+
+    def half_block(t, first, half):
+        return pl.ds(pl.multiple_of(t * RT + first * Q1 + half * QH, QH), QH)
+
+    def gather_a(j, t, n):
+        piece = err.at[core, j, piece_rows(t)]
+        return remote(piece, piece, ga_s.at[2 * j + t, n - 1], ga_r.at[2 * j + t, n - 1], at(core, a, turn(b, n)))
+
+    def gather_b(j, t, m):
+        rows, n = [
+            (block(t, a), 1),
+            (block(t, a), 3),
+            (half_block(t, turn(a, 3), 0), 1),
+            (half_block(t, turn(a, 1), 1), 3),
+        ][m]
+        piece = err.at[core, j, rows]
+        return remote(piece, piece, gb_s.at[2 * j + t, m], gb_r.at[2 * j + t, m], at(core, turn(a, n), b))
+
+    def gather_c(j, t, n):
+        piece = err.at[core, j, block(t, turn(a, n))]
+        return remote(piece, piece, gc_s.at[2 * j + t, n], gc_r.at[2 * j + t, n], sib_id)
+
+    def gather_1(j, t):
+        for n in (2, 1, 3):
+            gather_a(j, t, n).start()
+
+    def gather_2(j, t):
+        for n in (1, 3, 2):
+            gather_a(j, t, n).wait_recv()
+        gather_b(j, t, 0).start()
+        gather_b(j, t, 1).start()
+        gather_c(j, t, 0).start()
+
+    def gather_3(j, t):
+        gather_b(j, t, 0).wait_recv()
+        gather_b(j, t, 2).start()
+        gather_c(j, t, 3).start()
+        gather_b(j, t, 1).wait_recv()
+        gather_b(j, t, 3).start()
+        gather_c(j, t, 1).start()
+
+    def gather_4(j, t):
+        gather_b(j, t, 2).wait_recv()
+        gather_b(j, t, 3).wait_recv()
+        gather_c(j, t, 2).start()
+
+    def wait_error(j, t):
+        for n in (0, 1, 3, 2):
+            gather_c(j, t, n).wait_recv()
+
+    def each(stage, t):
+        stage(1, t)
+
+        @pl.when(low)
+        def _():
+            stage(0, t)
+
+    def target(stage, t):
+        @pl.when(away)
+        def _():
+            for h in range(2):
+                stage(2 * t + h)
+
+    def send_target(t):
+        @pl.when(away)
+        def _():
+            second_end(2 * t)
+            second_end(2 * t + 1)
+            tg_snd[t, 0] = fin[2 * t + core].astype(BF16)
+            tg_snd[t, 1] = fin[2 * t + 1 - core].astype(BF16)
+            tg_par(t).start()
+            tg_diag(t).start()
+
+    def send_slot_1(t):
+        second_end(unit(1, t))
+
+        @pl.when(jnp.logical_not(low))
+        def _():
+            take_target(1, t)
+
+        x_snd[t] = fin[unit(1, t)].astype(BF16)
+        x_copy(t).start()
+
+    def error_1(t):
+        x_copy(t).wait_recv()
+        write_error(1, t, fin[unit(1, t)] + x_rcv[t].astype(F32))
+        gather_1(1, t)
+
+    def error_0(t):
+        @pl.when(low)
+        def _():
+            second_end(unit(0, t))
+            take_target(0, t)
+            write_error(0, t, fin[unit(0, t)])
+            gather_1(0, t)
+
+    def relay_of(j, t):
+        ring_relay(unit(j, t))
+
+    def second_of_unit(j, t):
+        second_start(unit(j, t))
+
+    loads[4].wait()
+    mlp(0)
     activate(0)
     loads[5].wait()
-    recon(1, 0)
-
-    @pl.when(away)
-    def _():
-        ring_relay(0)
-        ring_relay(1)
-
+    each(recon, 0)
+    target(ring_relay, 0)
+    each(chip_sum, 0)
+    mlp(1)
+    target(second_start, 0)
+    each(relay_of, 0)
     activate(1)
-    recon(1, 1)
-
-    @pl.when(low)
-    def _():
-        recon(0, 0)
-
-    chip_sum(1)
-    ring_start(2)
-
-    @pl.when(away)
-    def _():
-        second_start(0)
-        second_start(1)
-
-    @pl.when(low)
-    def _():
-        recon(0, 1)
-
-    ring_relay(2)
-
-    @pl.when(low)
-    def _():
-        chip_sum(0)
-        ring_start(3)
-
-    @pl.when(away)
-    def _():
-        second_end(0)
-        second_end(1)
-        tg_snd[0] = fin[core].astype(BF16)
-        tg_snd[1] = fin[1 - core].astype(BF16)
-        tg_par.start()
-        tg_diag.start()
-
-    second_start(2)
-
-    @pl.when(low)
-    def _():
-        ring_relay(3)
-
-    second_end(2)
-    x_copy = remote(x_snd, x_rcv, x_s, x_r, xhi_id)
-    a, b = first_of(core), second_of(core)
-    my_rows = pl.ds(pl.multiple_of(a * Q1 + b * Q2, Q2), Q2)
-
-    def write_error(j, total):
-        bias = dbias_v[pl.ds(2 * j + par, 1), half_cols]
-        err[core, j, my_rows, :] = ((total + bias) * 0.0625).astype(BF16)
-
-    def take_target(u):
-        tg_par.wait_recv()
-        fin[u] = fin[u] - tg_rcv[...].astype(F32)
-
-    @pl.when(jnp.logical_not(low))
-    def _():
-        take_target(2)
-
-    x_snd[...] = fin[2].astype(BF16)
-    x_copy.start()
+    each(recon, 1)
+    each(second_of_unit, 0)
+    target(ring_relay, 1)
+    send_target(0)
+    each(chip_sum, 1)
+    send_slot_1(0)
+    error_0(0)
+    target(second_start, 1)
+    each(relay_of, 1)
+    error_1(0)
+
     act_t[...] = act[...].T
     for n in range(W // CT):
         cols = pl.ds(pl.multiple_of(par * W + n * CT, 128), CT)
         rows_t[pl.ds(n * CT, CT), :] = nrm[:, cols].T
     rows_copy.start()
 
-    @pl.when(low)
-    def _():
-        second_start(3)
-
-    def block(first):
-        return pl.ds(pl.multiple_of(first * Q1, Q1), Q1)
-
-    def gather_a(j, n):
-        piece = err.at[core, j, my_rows]
-        return remote(piece, piece, ga_s.at[j, n - 1], ga_r.at[j, n - 1], at(core, a, turn(b, n)))
-
-    def gather_b(j, m):
-        rows, n = [
-            (block(a), 1), (block(a), 3), (half_rows(turn(a, 3), 0), 1), (half_rows(turn(a, 1), 1), 3)
-        ][m]
-        piece = err.at[core, j, rows]
-        return remote(piece, piece, gb_s.at[j, m], gb_r.at[j, m], at(core, turn(a, n), b))
-
-    def gather_c(j, n):
-        piece = err.at[core, j, block(turn(a, n))]
-        return remote(piece, piece, gc_s.at[j, n], gc_r.at[j, n], sib_id)
-
-    def gather_1(j):
-        for n in (1, 2, 3):
-            gather_a(j, n).start()
-
-    def gather_2(j):
-        for n in (1, 2, 3):
-            gather_a(j, n).wait_recv()
-        gather_b(j, 0).start()
-        gather_b(j, 1).start()
-        gather_c(j, 0).start()
-
-    def gather_3(j):
-        gather_b(j, 0).wait_recv()
-        gather_b(j, 2).start()
-        gather_c(j, 3).start()
-        gather_b(j, 1).wait_recv()
-        gather_b(j, 3).start()
-        gather_c(j, 1).start()
-
-    def gather_4(j):
-        gather_b(j, 2).wait_recv()
-        gather_b(j, 3).wait_recv()
-        gather_c(j, 2).start()
-
-    def wait_error(j):
-        for n in range(4):
-            gather_c(j, n).wait_recv()
+    each(second_of_unit, 1)
+    send_target(1)
+    each(gather_2, 0)
+    send_slot_1(1)
+    error_0(1)
+    error_1(1)
+    each(gather_3, 0)
+    each(gather_2, 1)
+    each(gather_4, 0)
+    each(wait_error, 0)
 
     def back_tile(j, rows):
         out = None
@@ -415,34 +457,10 @@
 
     outs = [pltpu.make_async_copy(dg_v.at[j], dgrad_h.at[j], out_sem.at[j]) for j in range(2)]
 
-    x_copy.wait_recv()
-    write_error(1, fin[2] + x_rcv[...].astype(F32))
-    gather_1(1)
-
-    @pl.when(low)
-    def _():
-        second_end(3)
-        take_target(3)
-        write_error(0, fin[3])
-        gather_1(0)
-
-    gather_2(1)
-
-    @pl.when(low)
-    def _():
-        gather_2(0)
-
-    gather_3(1)
-
-    @pl.when(low)
-    def _():
-        gather_3(0)
-
-    gather_4(1)
-    wait_error(1)
-
-    def back_first(r):
-        rows = pl.ds(r * RT, RT)
+    bk_copy = []
+
+    def back_rows(r):
+        rows = pl.ds(r * BT, BT)
 
         @pl.when(live1)
         def _():
@@ -450,23 +468,7 @@
 
         @pl.when(jnp.logical_not(live1))
         def _():
-            back[rows, :] = jnp.zeros((RT, F), F32)
-
-    back_first(0)
-
-    @pl.when(low)
-    def _():
-        gather_4(0)
-
-    back_first(1)
-
-    @pl.when(low)
-    def _():
-        wait_error(0)
-
-    bk_copy = []
-    for r in range(T // BT):
-        rows = pl.ds(r * BT, BT)
+            back[rows, :] = jnp.zeros((BT, F), F32)
 
         @pl.when(live0)
         def _():
@@ -475,6 +477,14 @@
         bk_snd[rows, :] = back[rows, :].astype(BF16)
         bk_copy.append(remote(bk_snd.at[rows], bk_rcv.at[rows], bk_s.at[r], bk_r.at[r], par_id))
         bk_copy[r].start()
+
+    each(gather_3, 1)
+    for r in range(T // BT // 2):
+        back_rows(r)
+    each(gather_4, 1)
+    each(wait_error, 1)
+    for r in range(T // BT // 2, T // BT):
+        back_rows(r)
 
     for j, live in ((1, live1), (0, live0)):
 
@@ -506,34 +516,32 @@
     for copy in pre_copy + bk_copy:
         copy.wait_send()
 
-    def drain(u, j):
+    def drain(u):
         for m in range(6):
             ring(u, m).wait_send()
         for n in (1, 2, 3):
             second_copy(u, n).wait_send()
-        if j is not None:
-            for r in range(2):
-                core_copy(j, r).wait_send()
-            for n in (1, 2, 3):
-                gather_a(j, n).wait_send()
-            for n in range(4):
-                gather_b(j, n).wait_send()
-                gather_c(j, n).wait_send()
-
-    drain(2, 1)
-
-    @pl.when(low)
-    def _():
-        drain(3, 0)
+
+    def drain_slot(j, t):
+        drain(unit(j, t))
+        core_copy(j, t).wait_send()
+        for n in (1, 2, 3):
+            gather_a(j, t, n).wait_send()
+        for n in range(4):
+            gather_b(j, t, n).wait_send()
+            gather_c(j, t, n).wait_send()
+
+    for t in range(2):
+        each(drain_slot, t)
+        target(drain, t)
+        x_copy(t).wait_send()
 
     @pl.when(away)
     def _():
-        drain(0, None)
-        drain(1, None)
-        tg_par.wait_send()
-        tg_diag.wait_send()
-
-    x_copy.wait_send()
+        for t in range(2):
+            tg_par(t).wait_send()
+            tg_diag(t).wait_send()
+
     for copy in outs:
         copy.wait()
     rows_copy.wait()
@@ -597,16 +605,16 @@
         pltpu.VMEM((2, T, W), F32),
         pltpu.VMEM((2, T, W), BF16),
         pltpu.VMEM((2, T, W), BF16),
-        pltpu.VMEM((4, T, W), BF16),
-        pltpu.VMEM((4, 2, QH, W), BF16),
-        pltpu.VMEM((4, 6, QH, W), BF16),
-        pltpu.VMEM((4, 3, Q2, W), BF16),
-        pltpu.VMEM((4, 3, Q2, W), BF16),
-        pltpu.VMEM((4, Q2, W), F32),
+        pltpu.VMEM((8, RT, W), BF16),
+        pltpu.VMEM((8, 2, QH, W), BF16),
+        pltpu.VMEM((8, 6, QH, W), BF16),
+        pltpu.VMEM((8, 3, Q2, W), BF16),
+        pltpu.VMEM((8, 3, Q2, W), BF16),
+        pltpu.VMEM((8, Q2, W), F32),
+        pltpu.VMEM((2, 2, Q2, W), BF16),
         pltpu.VMEM((2, Q2, W), BF16),
-        pltpu.VMEM((Q2, W), BF16),
-        pltpu.VMEM((Q2, W), BF16),
-        pltpu.VMEM((Q2, W), BF16),
+        pltpu.VMEM((2, Q2, W), BF16),
+        pltpu.VMEM((2, Q2, W), BF16),
         pltpu.VMEM((2, 2, T, W), BF16),
         pltpu.VMEM((T, F), F32),
         pltpu.VMEM((T, F), BF16),
@@ -615,9 +623,9 @@
         pltpu.VMEM((2, F, D), BF16),
         dma((6,)), dma((4,)),
     ]
-    scratch += pair(2) + pair(2, 2) + pair(4, 6) + pair(4, 3)
-    scratch += [dma((2,)), dma, dma, dma]
-    scratch += pair(2, 3) + pair(2, 4) + pair(2, 4) + pair(T // BT)
+    scratch += pair(2) + pair(2, 2) + pair(8, 6) + pair(8, 3)
+    scratch += [dma((2, 2)), dma((2,))] + pair(2)
+    scratch += pair(4, 3) + pair(4, 4) + pair(4, 4) + pair(T // BT)
     rows, dpre, bsum, dgrad = pl.pallas_call(
         kernel,
         out_shape=(

time: 94.7 us -> 89.4 us (0.944)
  Pallas kernels: 93.9 us -> 88.6 us
    pallas_call x1, Pallas kernels: 86.7 us -> 81.4 us  [shards(): pl.pallas_call(kernel, out_shape=(jax.ShapeDtypeStruct((W, T), BF16), jax...]
where the time goes in v3:
time: 89.4 us; the launch traced here: 89.2 us
  Pallas kernels  88.6 us (99%)
    pallas_call x1, Pallas kernels, shards(): pl.pallas_call(kernel, out_shape=(jax.ShapeDtypeStruct((W, T), BF16), jax...  81.4 us
    pallas_call x1, Pallas kernels, shards(): pl.pallas_call(finish_kernel, out_shape=(jax.ShapeDtypeStruct((1, W, F),...  7.15 us

profile of v3, /device:TPU:1, one launch (start us, length us, event | category | flops | bytes accessed | tf_op | source)
XLA Modules:
  0.0 89.2 jit_solution(3294909653886742517)
XLA Ops:
  0.6 81.4 %shard_map.112 = (bf16[1152,512]{1,0:T(8,128)(2,1)}, bf16[512,512]{1,0:T(8,128)(2,1)}, f32[1,512]{1,0:T(1,128)}, bf16[2,512,2304]{2,1,0:T(8,128)(2,1)}) custom-call(bf16[1,512,2304]{2,1,0:T(8,128)(2,1)} %res_h.1, f32[1,2304]{1,0:T(1,128)} %gain_v.1, bf16[1,288,2304]{2,1,0:T(8,128)(2,1)} %bitcast.2, bf16[1,288,2304]{2,1,0:T(8,128)(2,1)} %bitcast.3, ...), custom_call_target="tpu_custom_call" | custom-call | tf_op jit(solution)/shard_map/pallas_call | solution.py:629
  82.1 7.2 %shard_map.113 = (f32[1,1152,512]{2,1,0:T(8,128)}, f32[1,512]{1,0:T(1,128)}, bf16[1,1,2,512,2304]{4,3,2,1,0:T(8,128)(2,1)}) custom-call(bf16[1152,512]{1,0:T(8,128)(2,1)} %get-tuple-element.7.rows_h, bf16[512,512]{1,0:T(8,128)(2,1)} %get-tuple-element.8.dpre_h, f32[1,512]{1,0:T(1,128)} %get-tuple-element.9.bsum_v, ...), custom_call_target="tpu_custom_call" | custom-call | tf_op jit(solution)/shard_map/pallas_call | solution.py:654

commit v4 on v3

--- a/solution.py
+++ b/solution.py
@@ -19,7 +19,7 @@
 QH = Q1 // 2
 Q2 = RT // 16
 CT = 384
-BT = 128
+BT = 256
 
 
 def kernel(
@@ -407,15 +407,9 @@
     each(chip_sum, 1)
     send_slot_1(0)
     error_0(0)
+    each(relay_of, 1)
     target(second_start, 1)
-    each(relay_of, 1)
     error_1(0)
-
-    act_t[...] = act[...].T
-    for n in range(W // CT):
-        cols = pl.ds(pl.multiple_of(par * W + n * CT, 128), CT)
-        rows_t[pl.ds(n * CT, CT), :] = nrm[:, cols].T
-    rows_copy.start()
 
     each(second_of_unit, 1)
     send_target(1)
@@ -425,6 +419,12 @@
     error_1(1)
     each(gather_3, 0)
     each(gather_2, 1)
+    act_t[...] = act[...].T
+    for n in range(W // CT):
+        cols = pl.ds(pl.multiple_of(par * W + n * CT, 128), CT)
+        rows_t[pl.ds(n * CT, CT), :] = nrm[:, cols].T
+    rows_copy.start()
+
     each(gather_4, 0)
     each(wait_error, 0)
 

time: 89.4 us -> 88 us (0.984)
  Pallas kernels: 88.6 us -> 87.2 us
    pallas_call x1, Pallas kernels: 81.4 us -> 80 us  [shards(): pl.pallas_call(kernel, out_shape=(jax.ShapeDtypeStruct((W, T), BF16), jax...]
where the time goes in v4:
time: 88 us; the launch traced here: 87.8 us
  Pallas kernels  87.2 us (99%)
    pallas_call x1, Pallas kernels, shards(): pl.pallas_call(kernel, out_shape=(jax.ShapeDtypeStruct((W, T), BF16), jax...  80 us
    pallas_call x1, Pallas kernels, shards(): pl.pallas_call(finish_kernel, out_shape=(jax.ShapeDtypeStruct((1, W, F),...  7.15 us

profile of v4, /device:TPU:1, one launch (start us, length us, event | category | flops | bytes accessed | tf_op | source)
XLA Modules:
  0.0 87.8 jit_solution(8300429916856879630)
XLA Ops:
  0.6 80.0 %shard_map.112 = (bf16[1152,512]{1,0:T(8,128)(2,1)}, bf16[512,512]{1,0:T(8,128)(2,1)}, f32[1,512]{1,0:T(1,128)}, bf16[2,512,2304]{2,1,0:T(8,128)(2,1)}) custom-call(bf16[1,512,2304]{2,1,0:T(8,128)(2,1)} %res_h.1, f32[1,2304]{1,0:T(1,128)} %gain_v.1, bf16[1,288,2304]{2,1,0:T(8,128)(2,1)} %bitcast.2, bf16[1,288,2304]{2,1,0:T(8,128)(2,1)} %bitcast.3, ...), custom_call_target="tpu_custom_call" | custom-call | tf_op jit(solution)/shard_map/pallas_call | solution.py:629
  80.7 7.2 %shard_map.113 = (f32[1,1152,512]{2,1,0:T(8,128)}, f32[1,512]{1,0:T(1,128)}, bf16[1,1,2,512,2304]{4,3,2,1,0:T(8,128)(2,1)}) custom-call(bf16[1152,512]{1,0:T(8,128)(2,1)} %get-tuple-element.7.rows_h, bf16[512,512]{1,0:T(8,128)(2,1)} %get-tuple-element.8.dpre_h, f32[1,512]{1,0:T(1,128)} %get-tuple-element.9.bsum_v, ...), custom_call_target="tpu_custom_call" | custom-call | tf_op jit(solution)/shard_map/pallas_call | solution.py:654
